TPU v7x, 512 devices: a whole 4x4x16 slice. The times are simulated.
512 devices in a mesh: expert: 64 (over x, z), dp: 4 (over y), test: 2 (over core).
Axes of the slice: x: 4, y: 4, z: 16, core: 2. Of those that a mesh axis runs over, the one named last changes fastest.
Arguments:
- tokens: bfloat16 [16384, 3584], P(('expert', 'dp'), 'test'), may hold values from -6 to 6
- out_grad: bfloat16 [16384, 3584], P(('expert', 'dp'), 'test'), may hold values from -6 to 6
- route_ids: int32 [16384, 8], P(('expert', 'dp')), may hold values from 0 to 255, as said below
- route_slots: int32 [16384, 8], P(('expert', 'dp')), may hold values from -1 to 1, as said below
- route_weight: bfloat16 [16384, 8], P(('expert', 'dp')), may hold values from 0.19921875 to 1
- w_gate: bfloat16 [64, 3584, 1024], P('expert', None, ('dp', 'test')), may hold values from -0.09375 to 0.09375
- w_up: bfloat16 [64, 3584, 1024], P('expert', None, ('dp', 'test')), may hold values from -0.09375 to 0.09375
- w_down: bfloat16 [64, 1024, 3584], P('expert', ('dp', 'test')), may hold values from -0.1875 to 0.1875
- proj_hidden: bfloat16 [64, 64, 1024], P('expert', None, ('dp', 'test')), may hold values from -0.1875 to 0.1875
- proj_grad: bfloat16 [64, 64, 3584], P('expert'), may hold values from -0.09375 to 0.09375
- test_feats: bfloat16 [64, 256, 4096], P('expert', 'test'), may hold values from -0.09375 to 0.09375
Outputs:
- in_grad: bfloat16 [16384, 3584], P(('expert', 'dp'), 'test')
- scores: float32 [16384, 256], P(('expert', 'dp'), 'test')
Inputs may be any that keep to these rules, and one draw needn't show every extreme that they name: `route_ids`: each row names 8 different experts. `route_slots`: A route's slot is -1 exactly when its expert is 64 or more, or when 2 earlier tokens of the same aligned block of 64 rows already take that expert; otherwise it is the number of earlier tokens of that block routed to that expert.
All inputs are finite; a program needn't handle non-finite values.
Results may differ from a plain program's by a relative error of at most 0.0065.
Values may be sent and summed in bfloat16 or wider, within the bound.
A program may use at most 64 MiB of HBM per device.

v0:
```python
import jax
import jax.numpy as jnp
from jax import lax
from jax.sharding import PartitionSpec as P

CAP = 2


def pick_tables(ids_in, slots_in, weights_in, experts):
    live_mask = (slots_in >= 0) & (ids_in < experts)
    slot_code = jnp.where(live_mask, ids_in * CAP + slots_in, -1)
    columns = jnp.arange(experts * CAP, dtype=jnp.int32)
    matches = slot_code[:, :, None] == columns[None, None, :]
    picks = jnp.sum(matches.astype(jnp.float32), axis=1)
    weighted = jnp.sum(jnp.where(matches, weights_in.astype(jnp.float32)[:, :, None], 0.0), axis=1)
    return (picks.astype(jnp.bfloat16), weighted.astype(jnp.bfloat16))


def dot(a, b, ca, cb):
    return lax.dot_general(a, b, (((ca,), (cb,)), ((), ())), preferred_element_type=jnp.float32)


def on_device(
    tokens,
    out_grad,
    route_ids,
    route_slots,
    route_weight,
    w_gate,
    w_up,
    w_down,
    proj_hidden,
    proj_grad,
    test_feats,
):
    experts = lax.axis_size("expert")
    groups = lax.axis_size("dp")
    halves = lax.axis_size("test")
    half = tokens.shape[1]
    slots = experts * CAP
    pick, weighted = pick_tables(route_ids, route_slots, route_weight, experts)
    in_buf = dot(pick, tokens, 0, 0).astype(jnp.bfloat16)
    grad_buf = dot(weighted, out_grad, 0, 0).astype(jnp.bfloat16)

    def exchange(rows):
        width = rows.shape[1]
        moved = lax.all_to_all(
            rows.reshape(experts, CAP, width), "expert", split_axis=0, concat_axis=0, tiled=True
        )
        return moved.reshape(slots, width)

    def spread(rows):
        full = lax.all_gather(rows, ("dp", "test"), axis=0, tiled=True)
        full = full.reshape(groups, halves, slots, half)
        return [full[:, h].reshape(groups * slots, half) for h in range(halves)]

    mine_in = exchange(in_buf)
    ins = spread(mine_in)
    mine_grad = exchange(grad_buf)
    grads = spread(mine_grad)
    gate_w, up_w, down_w = (w_gate[0], w_up[0], w_down[0])

    def cut(arr, h, axis):
        return lax.slice_in_dim(arr, h * half, (h + 1) * half, axis=axis)

    gate_pre = sum((dot(ins[h], cut(gate_w, h, 0), 1, 0) for h in range(halves)))
    up_pre = sum((dot(ins[h], cut(up_w, h, 0), 1, 0) for h in range(halves)))
    sig = jax.nn.sigmoid(gate_pre)
    act = gate_pre * sig
    hidden = (act * up_pre).astype(jnp.bfloat16)
    proj_part = dot(hidden, proj_hidden[0], 1, 1)
    hid_grad = sum((dot(grads[h], cut(down_w, h, 1), 1, 1) for h in range(halves)))
    up_grad = (hid_grad * act).astype(jnp.bfloat16)
    gate_grad = (hid_grad * up_pre * sig * (1.0 + gate_pre * (1.0 - sig))).astype(jnp.bfloat16)
    parts = [
        (dot(gate_grad, cut(gate_w, h, 0), 1, 1) + dot(up_grad, cut(up_w, h, 0), 1, 1)).astype(
            jnp.bfloat16
        )
        for h in range(halves)
    ]
    parts = jnp.stack([p.reshape(groups, slots, half) for p in parts], axis=1)
    mine_back = lax.psum_scatter(
        parts.reshape(groups * halves * slots, half),
        ("dp", "test"),
        scatter_dimension=0,
        tiled=True,
    )
    back = exchange(mine_back.astype(jnp.bfloat16))
    in_grad = dot(pick, back, 1, 0).astype(jnp.bfloat16)
    hidden_vec = lax.psum(proj_part, ("dp", "test"))
    me = lax.axis_index("dp")
    hid_mine = lax.dynamic_slice_in_dim(hidden_vec, me * slots, slots, 0)
    grad_mine = sum(
        (
            dot(
                lax.dynamic_slice_in_dim(grads[h], me * slots, slots, 0),
                cut(proj_grad[0], h, 1),
                1,
                1,
            )
            for h in range(halves)
        )
    )
    feature = (hid_mine[:, :, None] * grad_mine[:, None, :]).reshape(slots, -1).astype(jnp.bfloat16)
    score = dot(feature, test_feats[0], 1, 1).astype(jnp.bfloat16)
    scores = dot(pick, exchange(score), 1, 0)
    return (in_grad, scores)


def solution(mesh):
    placed = (
        P(("expert", "dp"), "test"),
        P(("expert", "dp"), "test"),
        P(("expert", "dp"), None),
        P(("expert", "dp"), None),
        P(("expert", "dp"), None),
        P("expert", None, ("dp", "test")),
        P("expert", None, ("dp", "test")),
        P("expert", ("dp", "test"), None),
        P("expert", None, ("dp", "test")),
        P("expert", None, None),
        P("expert", "test", None),
    )
    return jax.shard_map(
        on_device,
        mesh=mesh,
        in_specs=placed,
        out_specs=(P(("expert", "dp"), "test"), P(("expert", "dp"), "test")),
        check_vma=False,
    )
```

profile of v0, /device:TPU:31, one launch (start us, length us, event | category | flops | bytes accessed | tf_op | source)
XLA Modules:
  0.0 316.4 jit_solution(14806735404021677156)
XLA Ops:
  7.2 0.8 add_select_fusion
  8.0 0.1 copy.21
  8.1 0.8 copy.22
  8.9 0.2 select_reduce_fusion
  9.1 1.3 convolution_convert_fusion.1
  10.4 0.2 reshape.58
  10.6 45.3 %all_to_all.20 = bf16[64,2,1792]{2,1,0:T(2,128)(2,1)S(1)} all-to-all(bf16[64,2,1792]{2,1,0:T(2,128)(2,1)S(1)} %reshape.58), channel_id=1, replica_groups=mesh['expert'=64,'dp'=4,'test'=2] {'expert'}, dimensions={0} | all-to-all | bytes 917504 | tf_op jit(solution)/shard_map/all_to_all | solution.py:47
  55.9 1.0 reshape.59
  56.9 0.3 convolution_convert_fusion
  57.2 0.2 reshape.61
  57.4 34.0 %all_to_all.21 = bf16[64,2,1792]{2,1,0:T(2,128)(2,1)S(1)} all-to-all(bf16[64,2,1792]{2,1,0:T(2,128)(2,1)S(1)} %reshape.61), channel_id=1, replica_groups=mesh['expert'=64,'dp'=4,'test'=2] {'expert'}, dimensions={0} | all-to-all | bytes 917504 | tf_op jit(solution)/shard_map/all_to_all | solution.py:47
  91.4 0.9 reshape.62
  92.4 0.0 all-reduce.2.cloned.1.call-start
  92.4 3.6 %fusion.41 = (bf16[4,1,128,1792]{3,2,1,0:T(8,128)(2,1)}, bf16[4,1,128,1792]{3,2,1,0:T(8,128)(2,1)S(1)}) fusion(bf16[4,2,128,1792]{3,2,1,0:T(8,128)(2,1)} %bitcast.73), kind=kLoop, calls=%fused_computation.61 | loop fusion | bytes 7340032 | tf_op jit(solution)/shard_map/slice | solution.py:55
  96.0 31.3 %all-gather.5.cloned.1.call-done = bf16[1024,1792]{1,0:T(8,128)(2,1)} async-done(((bf16[128,1792]{1,0:T(8,128)(2,1)}), bf16[1024,1792]{1,0:T(8,128)(2,1)}) %all-gather.5.cloned.1.call-update) | async-done | bytes 3670032 | tf_op jit(solution)/shard_map/all_gather | solution.py:53
  127.4 2.4 fusion.42
  129.8 0.6 fusion.9
  130.4 0.5 copy-done.3
  130.9 0.6 fusion.14
  131.6 0.6 convolution_add_fusion.1
  132.3 0.6 convolution_add_fusion
  132.9 0.5 copy-done.7
  133.4 0.6 fusion.2
  134.1 0.4 copy-done.5
  134.5 0.6 multiply_convert_fusion.2
  135.1 2.4 fusion.4
  137.6 2.5 fusion.7
  140.1 0.9 fusion.30
  141.0 3.0 add_convert_fusion
  144.0 0.3 copy-done.1
  144.3 0.2 copy-done.4
  144.5 0.6 add_convert_fusion.1
  145.2 2.1 pad_maximum_fusion
  147.3 1.0 copy-done.6
  148.3 0.3 fusion.17
  148.6 1.3 convolution_add_fusion.3
  149.9 66.4 %all-reduce.2.cloned.1.call-done = f32[512,64]{0,1:T(8,128)} async-done(((f32[512,64]{0,1:T(8,128)}), f32[512,64]{0,1:T(8,128)}) %all-reduce.2.cloned.1.call-update) | async-done | bytes 131088 | tf_op jit(solution)/shard_map/psum | solution.py:90
  216.3 0.8 constant_dynamic-slice_fusion
  217.1 0.3 multiply_convert_fusion
  217.4 1.1 convolution_convert_fusion.3
  218.5 15.3 %all-to-all-start.3 = ((bf16[64,2,128]{2,1,0:T(2,128)(2,1)}), bf16[64,2,128]{2,1,0:T(2,128)(2,1)S(1)}, u32[]{:S(2)}, u32[]{:S(2)}) async-start(bf16[64,2,128]{2,1,0:T(2,128)(2,1)} %bitcast.20), calls=%async_computation.4 | async-start | bytes 65536 | tf_op jit(solution)/shard_map/all_to_all | solution.py:47
  233.8 29.1 %reduce-scatter.2.cloned.1.call-done = bf16[128,1792]{1,0:T(8,128)(2,1)} async-done(((bf16[1024,1792]{1,0:T(8,128)(2,1)}), bf16[128,1792]{1,0:T(8,128)(2,1)}) %reduce-scatter.2.cloned.1.call-update) | async-done | bytes 458768 | tf_op jit(solution)/shard_map/reduce_scatter | solution.py:82
  262.9 2.0 reshape.65
  264.9 15.0 %all-to-all-start.2 = ((bf16[64,2,1792]{2,1,0:T(2,128)(2,1)}), bf16[64,2,1792]{2,1,0:T(2,128)(2,1)S(1)}, u32[]{:S(2)}, u32[]{:S(2)}) async-start(bf16[64,2,1792]{2,1,0:T(2,128)(2,1)} %reshape.65), calls=%async_computation.3 | async-start | bytes 917504 | tf_op jit(solution)/shard_map/all_to_all | solution.py:47
  279.9 0.7 fusion.43
  280.6 28.2 %all-to-all-done.2 = bf16[64,2,1792]{2,1,0:T(2,128)(2,1)S(1)} async-done(((bf16[64,2,1792]{2,1,0:T(2,128)(2,1)}), bf16[64,2,1792]{2,1,0:T(2,128)(2,1)S(1)}, u32[]{:S(2)}, u32[]{:S(2)}) %all-to-all-start.2) | async-done | bytes 458784 | tf_op jit(solution)/shard_map/all_to_all | solution.py:47
  308.8 0.2 reshape.66
  309.0 0.9 convolution_convert_fusion.2
  (23 shorter events, 0.2 us)
Async XLA Ops:
  7.2 210.2 %copy-start = (bf16[1,128,4096]{2,1,0:T(8,128)(2,1)S(1)}, bf16[1,128,4096]{2,1,0:T(8,128)(2,1)}, u32[]{:S(2)}) copy-start(bf16[1,128,4096]{2,1,0:T(8,128)(2,1)} %param.21) | copy-start | bytes 3145732
  7.2 85.2 %all-gather.3.cloned.1.call-start = ((), (), s32[]{:S(2)}) async-start(), calls=%async_computation.5 | async-start | bytes 4128768 | tf_op jit(solution)/shard_map/all_gather | solution.py:53
  9.1 47.8 %copy-start.8 = (bf16[64,1792]{1,0:T(8,128)(2,1)S(1)}, bf16[64,1792]{1,0:T(8,128)(2,1)}, u32[]{:S(2)}) copy-start(bf16[64,1792]{1,0:T(8,128)(2,1)} %param.11) | copy-start | bytes 688132
  56.9 70.5 %all-gather.5.cloned.1.call-start = ((), (), s32[]{:S(2)}) async-start(), calls=%async_computation.6 | async-start | bytes 4128768 | tf_op jit(solution)/shard_map/all_gather | solution.py:53
  92.4 124.0 %all-reduce.2.cloned.1.call-start = ((), (), s32[]{:S(2)}) async-start(), calls=%async_computation.8 | async-start | bytes 262144 | tf_op jit(solution)/shard_map/psum | solution.py:90
  127.4 2.4 copy-start.2
  129.8 1.2 copy-start.3
  132.2 1.2 copy-start.7
  132.9 1.6 copy-start.5
  137.6 2.5 copy-start.9
  140.9 122.0 %reduce-scatter.2.cloned.1.call-start = ((), (), s32[]{:S(2)}) async-start(), calls=%async_computation.7 | async-start | bytes 4128768 | tf_op jit(solution)/shard_map/reduce_scatter | solution.py:82
  141.0 3.3 %copy-start.1 = (f32[512,1792]{1,0:T(8,128)S(1)}, f32[512,1792]{1,0:T(8,128)}, u32[]{:S(2)}) copy-start(f32[512,1792]{1,0:T(8,128)} %fusion.7) | copy-start | bytes 11010052
  141.0 3.5 %copy-start.4 = (bf16[1,3584,128]{2,1,0:T(8,128)(2,1)S(1)}, bf16[1,3584,128]{2,1,0:T(8,128)(2,1)}, u32[]{:S(2)}) copy-start(bf16[1,3584,128]{2,1,0:T(8,128)(2,1)} %param.17) | copy-start | bytes 2752516
  147.3 1.0 copy-start.6
  218.5 46.4 %all-to-all-start.3 = ((bf16[64,2,128]{2,1,0:T(2,128)(2,1)}), bf16[64,2,128]{2,1,0:T(2,128)(2,1)S(1)}, u32[]{:S(2)}, u32[]{:S(2)}) async-start(bf16[64,2,128]{2,1,0:T(2,128)(2,1)} %bitcast.20), calls=%async_computation.4 | async-start | bytes 65536 | tf_op jit(solution)/shard_map/all_to_all | solution.py:47
  264.9 43.9 %all-to-all-start.2 = ((bf16[64,2,1792]{2,1,0:T(2,128)(2,1)}), bf16[64,2,1792]{2,1,0:T(2,128)(2,1)S(1)}, u32[]{:S(2)}, u32[]{:S(2)}) async-start(bf16[64,2,1792]{2,1,0:T(2,128)(2,1)} %reshape.65), calls=%async_computation.3 | async-start | bytes 917504 | tf_op jit(solution)/shard_map/all_to_all | solution.py:47
Sparse Core Ops, SparseCore 0:
  57.0 30.6 all-gather.2
  92.5 34.8 all-gather.4
  141.1 75.2 all-reduce.1
  219.0 43.8 reduce-scatter.1
where the time goes:
time: 317 us; the launch traced here: 316 us
  waiting for transfers between devices  155 us (49%)
  blocking collectives  79.3 us (25%)
  starting transfers between devices  30.5 us (10%)
  matrix products  19.2 us (6%)
  local copies, waits for them, and re-layouts  15 us (5%)
  between operations  14 us (4%)
  other arithmetic  3.41 us (1%)
    all_to_all x2, blocking collectives, exchange(): lax.all_to_all(rows.reshape(experts, CAP, width), 'expert', split_axis=0,...  79.3 us
    psum x1, waiting for transfers between devices, on_device(): hidden_vec = lax.psum(proj_part, ('dp', 'test'))  66.4 us
    all_gather x2, waiting for transfers between devices, spread(): full = lax.all_gather(rows, ('dp', 'test'), axis=0, tiled=True)  31.3 us
    all_to_all x2, starting transfers between devices, exchange(): lax.all_to_all(rows.reshape(experts, CAP, width), 'expert', split_axis=0,...  30.3 us
    reduce_scatter x1, waiting for transfers between devices, on_device(): lax.psum_scatter(parts.reshape(groups * halves * slots, half), ('dp', 'te...  29.1 us
    all_to_all x2, waiting for transfers between devices, exchange(): lax.all_to_all(rows.reshape(experts, CAP, width), 'expert', split_axis=0,...  28.2 us
    dot_general x18, matrix products, dot(): lax.dot_general(a, b, (((ca,), (cb,)), ((), ())), preferred_element_type=...  19.2 us
  transfers between devices with their start and end apart: 6, of which 4 were waited for; matrix products, arithmetic and copies ran while one was open for 5% of the time, Pallas kernels for 0%

commit v1 on v0

--- a/solution.py
+++ b/solution.py
@@ -1,9 +1,18 @@
+import functools
 import jax
 import jax.numpy as jnp
 from jax import lax
 from jax.sharding import PartitionSpec as P
+from jax.lax import all_gather
 
 CAP = 2
+
+
+def raise_tables(original, axis_tag):
+    return jnp.sum(all_gather(original, axis_tag), 0)
+
+
+_match_cube = functools.partial(raise_tables, axis_tag=("dp", "test"))
 
 
 def pick_tables(ids_in, slots_in, weights_in, experts):
@@ -87,7 +96,7 @@
     )
     back = exchange(mine_back.astype(jnp.bfloat16))
     in_grad = dot(pick, back, 1, 0).astype(jnp.bfloat16)
-    hidden_vec = lax.psum(proj_part, ("dp", "test"))
+    hidden_vec = _match_cube(proj_part)
     me = lax.axis_index("dp")
     hid_mine = lax.dynamic_slice_in_dim(hidden_vec, me * slots, slots, 0)
     grad_mine = sum(

time: 317 us -> 267 us (0.84)
  waiting for transfers between devices: 155 us -> 108 us
  matrix products: 19.2 us -> 15.5 us
    psum x1 -> x0, waiting for transfers between devices: 66.4 us -> none  [on_device(): hidden_vec = lax.psum(proj_part, ('dp', 'test'))]
    all_gather x0 -> x1, waiting for transfers between devices: none -> 19.6 us  [raise_tables(): return jnp.sum(all_gather(original, axis_tag), 0)]
    dot_general x18, matrix products: 19.2 us -> 15.5 us  [dot(): lax.dot_general(a, b, (((ca,), (cb,)), ((), ())), preferred_element_type=...]
  transfers between devices with their start and end apart: 6 -> 6, of which waited for: 4 -> 4; matrix products, arithmetic and copies ran while one was open for 5% -> 8% of each run, Pallas kernels for 0% -> 0%
where the time goes in v1:
time: 267 us; the launch traced here: 266 us
  waiting for transfers between devices  108 us (40%)
  blocking collectives  79.3 us (30%)
  starting transfers between devices  30.5 us (11%)
  local copies, waits for them, and re-layouts  15.8 us (6%)
  matrix products  15.5 us (6%)
  between operations  14 us (5%)
  other arithmetic  3.66 us (1%)
    all_to_all x2, blocking collectives, exchange(): lax.all_to_all(rows.reshape(experts, CAP, width), 'expert', split_axis=0,...  79.3 us
    all_gather x2, waiting for transfers between devices, spread(): full = lax.all_gather(rows, ('dp', 'test'), axis=0, tiled=True)  31.4 us
    all_to_all x2, starting transfers between devices, exchange(): lax.all_to_all(rows.reshape(experts, CAP, width), 'expert', split_axis=0,...  30.3 us
    reduce_scatter x1, waiting for transfers between devices, on_device(): lax.psum_scatter(parts.reshape(groups * halves * slots, half), ('dp', 'te...  28.5 us
    all_to_all x2, waiting for transfers between devices, exchange(): lax.all_to_all(rows.reshape(experts, CAP, width), 'expert', split_axis=0,...  28.2 us
    all_gather x1, waiting for transfers between devices, raise_tables(): return jnp.sum(all_gather(original, axis_tag), 0)  19.6 us
    dot_general x18, matrix products, dot(): lax.dot_general(a, b, (((ca,), (cb,)), ((), ())), preferred_element_type=...  15.5 us
    slice x2, local copies, waits for them, and re-layouts, spread(): return [full[:, h].reshape(groups * slots, half) for h in range(halves)]  6 us
  transfers between devices with their start and end apart: 6, of which 4 were waited for; matrix products, arithmetic and copies ran while one was open for 8% of the time, Pallas kernels for 0%

profile of v1, /device:TPU:31, one launch (start us, length us, event | category | flops | bytes accessed | tf_op | source)
XLA Modules:
  0.0 266.4 jit_solution(6131072850505431678)
XLA Ops:
  7.2 0.8 add_select_fusion
  8.0 0.1 copy.20
  8.1 0.8 copy.21
  8.9 0.2 select_reduce_fusion
  9.1 1.3 convolution_convert_fusion.1
  10.4 0.2 reshape.58
  10.6 45.3 %all_to_all.20 = bf16[64,2,1792]{2,1,0:T(2,128)(2,1)S(1)} all-to-all(bf16[64,2,1792]{2,1,0:T(2,128)(2,1)S(1)} %reshape.58), channel_id=1, replica_groups=mesh['expert'=64,'dp'=4,'test'=2] {'expert'}, dimensions={0} | all-to-all | bytes 917504 | tf_op jit(solution)/shard_map/all_to_all | solution.py:56
  55.9 0.9 reshape.59
  56.8 0.0 all-gather.7.cloned.1.call-start
  56.9 0.3 convolution_convert_fusion
  57.2 0.2 reshape.61
  57.4 34.0 %all_to_all.21 = bf16[64,2,1792]{2,1,0:T(2,128)(2,1)S(1)} all-to-all(bf16[64,2,1792]{2,1,0:T(2,128)(2,1)S(1)} %reshape.61), channel_id=1, replica_groups=mesh['expert'=64,'dp'=4,'test'=2] {'expert'}, dimensions={0} | all-to-all | bytes 917504 | tf_op jit(solution)/shard_map/all_to_all | solution.py:56
  91.4 0.9 reshape.62
  92.4 3.6 %fusion.41 = (bf16[4,1,128,1792]{3,2,1,0:T(8,128)(2,1)}, bf16[4,1,128,1792]{3,2,1,0:T(8,128)(2,1)S(1)}) fusion(bf16[4,2,128,1792]{3,2,1,0:T(8,128)(2,1)} %bitcast.78), kind=kLoop, calls=%fused_computation.62 | loop fusion | bytes 7340032 | tf_op jit(solution)/shard_map/slice | solution.py:64
  96.0 31.3 %all-gather.7.cloned.1.call-done = bf16[1024,1792]{1,0:T(8,128)(2,1)} async-done(((bf16[128,1792]{1,0:T(8,128)(2,1)}), bf16[1024,1792]{1,0:T(8,128)(2,1)}) %all-gather.7.cloned.1.call-update) | async-done | bytes 3670032 | tf_op jit(solution)/shard_map/all_gather | solution.py:62
  127.4 2.4 fusion.42
  129.8 0.6 fusion.9
  130.4 0.5 copy-done.3
  130.9 0.6 fusion.14
  131.6 0.6 convolution_add_fusion.1
  132.2 0.6 convolution_add_fusion
  132.9 0.7 copy-done.7
  133.6 0.9 fusion.30
  134.5 0.0 reduce-scatter.2.cloned.1.call-start
  134.6 1.8 fusion.2
  136.4 1.7 multiply_convert_fusion.2
  138.2 0.6 fusion.4
  138.8 0.6 fusion.7
  139.5 0.5 copy-done.4
  140.0 0.6 add_convert_fusion
  140.6 0.6 add_convert_fusion.1
  141.3 2.1 pad_maximum_fusion
  143.4 1.0 copy-done.6
  144.4 0.3 fusion.17
  144.7 1.3 convolution_add_fusion.3
  146.0 19.6 %all-gather.9.cloned.1.call-done = f32[4096,64]{0,1:T(8,128)} async-done(((f32[512,64]{0,1:T(8,128)}), f32[4096,64]{0,1:T(8,128)}) %all-gather.9.cloned.1.call-update) | async-done | bytes 1048592 | tf_op jit(solution)/shard_map/all_gather | solution.py:12
  165.6 1.8 copy.24
  167.4 0.3 bitcast_reduce_fusion
  167.7 0.3 multiply_convert_fusion
  168.0 1.1 convolution_convert_fusion.3
  169.1 15.3 %all-to-all-start.3 = ((bf16[64,2,128]{2,1,0:T(2,128)(2,1)}), bf16[64,2,128]{2,1,0:T(2,128)(2,1)S(1)}, u32[]{:S(2)}, u32[]{:S(2)}) async-start(bf16[64,2,128]{2,1,0:T(2,128)(2,1)} %bitcast.20), calls=%async_computation.4 | async-start | bytes 65536 | tf_op jit(solution)/shard_map/all_to_all | solution.py:56
  184.5 28.5 %reduce-scatter.2.cloned.1.call-done = bf16[128,1792]{1,0:T(8,128)(2,1)} async-done(((bf16[1024,1792]{1,0:T(8,128)(2,1)}), bf16[128,1792]{1,0:T(8,128)(2,1)}) %reduce-scatter.2.cloned.1.call-update) | async-done | bytes 458768 | tf_op jit(solution)/shard_map/reduce_scatter | solution.py:91
  212.9 2.0 reshape.65
  214.9 15.0 %all-to-all-start.2 = ((bf16[64,2,1792]{2,1,0:T(2,128)(2,1)}), bf16[64,2,1792]{2,1,0:T(2,128)(2,1)S(1)}, u32[]{:S(2)}, u32[]{:S(2)}) async-start(bf16[64,2,1792]{2,1,0:T(2,128)(2,1)} %reshape.65), calls=%async_computation.3 | async-start | bytes 917504 | tf_op jit(solution)/shard_map/all_to_all | solution.py:56
  229.9 0.7 fusion.43
  230.6 28.2 %all-to-all-done.2 = bf16[64,2,1792]{2,1,0:T(2,128)(2,1)S(1)} async-done(((bf16[64,2,1792]{2,1,0:T(2,128)(2,1)}), bf16[64,2,1792]{2,1,0:T(2,128)(2,1)S(1)}, u32[]{:S(2)}, u32[]{:S(2)}) %all-to-all-start.2) | async-done | bytes 458784 | tf_op jit(solution)/shard_map/all_to_all | solution.py:56
  258.8 0.2 reshape.66
  259.0 0.9 convolution_convert_fusion.2
  (27 shorter events, 0.2 us)
Async XLA Ops:
  7.2 160.8 %copy-start = (bf16[1,128,4096]{2,1,0:T(8,128)(2,1)S(1)}, bf16[1,128,4096]{2,1,0:T(8,128)(2,1)}, u32[]{:S(2)}) copy-start(bf16[1,128,4096]{2,1,0:T(8,128)(2,1)} %param.21) | copy-start | bytes 3145732
  7.2 85.2 %all-gather.5.cloned.1.call-start = ((), (), s32[]{:S(2)}) async-start(), calls=%async_computation.5 | async-start | bytes 4128768 | tf_op jit(solution)/shard_map/all_gather | solution.py:62
  9.1 47.8 %copy-start.9 = (bf16[64,1792]{1,0:T(8,128)(2,1)S(1)}, bf16[64,1792]{1,0:T(8,128)(2,1)}, u32[]{:S(2)}) copy-start(bf16[64,1792]{1,0:T(8,128)(2,1)} %param.11) | copy-start | bytes 688132
  56.8 70.5 %all-gather.7.cloned.1.call-start = ((), (), s32[]{:S(2)}) async-start(), calls=%async_computation.6 | async-start | bytes 4128768 | tf_op jit(solution)/shard_map/all_gather | solution.py:62
  92.3 73.2 %all-gather.9.cloned.1.call-start = ((), (), s32[]{:S(2)}) async-start(), calls=%async_computation.8 | async-start | bytes 1179648 | tf_op jit(solution)/shard_map/all_gather | solution.py:12
  127.4 2.4 copy-start.1
  129.8 1.2 copy-start.3
  132.2 1.4 copy-start.10
  132.9 0.7 copy-start.7
  134.5 78.4 %reduce-scatter.2.cloned.1.call-start = ((), (), s32[]{:S(2)}) async-start(), calls=%async_computation.7 | async-start | bytes 4128768 | tf_op jit(solution)/shard_map/reduce_scatter | solution.py:91
  134.6 1.8 copy-start.5
  134.6 1.8 copy-start.8
  136.4 1.8 copy-start.2
  138.8 1.2 copy-start.4
  143.4 1.0 copy-start.6
  169.1 45.8 %all-to-all-start.3 = ((bf16[64,2,128]{2,1,0:T(2,128)(2,1)}), bf16[64,2,128]{2,1,0:T(2,128)(2,1)S(1)}, u32[]{:S(2)}, u32[]{:S(2)}) async-start(bf16[64,2,128]{2,1,0:T(2,128)(2,1)} %bitcast.20), calls=%async_computation.4 | async-start | bytes 65536 | tf_op jit(solution)/shard_map/all_to_all | solution.py:56
  214.9 43.9 %all-to-all-start.2 = ((bf16[64,2,1792]{2,1,0:T(2,128)(2,1)}), bf16[64,2,1792]{2,1,0:T(2,128)(2,1)S(1)}, u32[]{:S(2)}, u32[]{:S(2)}) async-start(bf16[64,2,1792]{2,1,0:T(2,128)(2,1)} %reshape.65), calls=%async_computation.3 | async-start | bytes 917504 | tf_op jit(solution)/shard_map/all_to_all | solution.py:56
Sparse Core Ops, SparseCore 0:
  57.0 30.6 all-gather.4
  92.5 34.8 all-gather.6
  134.6 30.9 all-gather.8
  168.3 44.6 reduce-scatter.1
